TPU v7x, 256 devices: a whole 4x4x8 slice. The times are simulated.
256 devices in a mesh: grp: 8 (over z), blk: 32 (over y, x, core).
Axes of the slice: x: 4, y: 4, z: 8, core: 2. Of those that a mesh axis runs over, the one named last changes fastest.
Arguments:
- embeddings: bfloat16 [8, 2048, 1024], P('grp', 'blk'), may hold values from -72 to 72
- cluster_ids: int32 [8, 2048], P('grp', 'blk'), may hold values from 0 to 63, never falling along the last dimension, each value on 1 to 128 neighbouring positions
- block_list: int32 [8, 256, 2], P('grp', 'blk'), may hold values from 0 to 31, as said below
- block_counts: int32 [8, 32], P('grp', 'blk'), may hold values from 1 to 8, as said below
- pair_targets: float32 [8, 256, 4096], P('grp', 'blk'), may hold values from -6 to 6
- w_left: bfloat16 [1024, 512], replicated, may hold values from -0.125 to 0.125
- w_right: bfloat16 [1024, 512], replicated, may hold values from -0.125 to 0.125
- hidden_bias: float32 [512], replicated, may hold values from -3 to 3
- w_middle: bfloat16 [512, 128], replicated, may hold values from -0.25 to 0.25
- w_final: float32 [128], replicated, may hold values from -0.5 to 0.5
Outputs:
- grad_embeddings: float32 [8, 2048, 1024], P('grp', 'blk')
- grad_left: float32 [1024, 512], replicated
- grad_right: float32 [1024, 512], replicated
- grad_bias: float32 [512], replicated
- grad_middle: float32 [512, 128], replicated
- grad_final: float32 [128], replicated
Inputs may be any that keep to these rules, and one draw needn't show every extreme that they name: `block_list`: entries are panels of the device's own group; the column panel lies within one of the row panel. `block_counts`: slots of a device at and beyond its count are unused; in every group one device has exactly 8.
All inputs are finite; a program needn't handle non-finite values.
Results may differ from a plain program's by a relative error of at most 0.012.
Values may be sent and summed in bfloat16 or wider, within the bound.
No kernel may reach another device: no remote copies, remote signals or barrier semaphores. Data moves between devices by JAX's collectives and lax.ppermute only.
A program may use at most 128 MiB of HBM per device.

v0:
```python
import math
import jax
import jax.numpy as jnp
from jax import lax
from jax.sharding import PartitionSpec as P

PANEL = 64
B_DEV = 8


def silu_slope(value):
    sigmoid_value = jax.nn.sigmoid(value)
    return sigmoid_value * (1.0 + value * (1.0 - sigmoid_value))


def pair_block(
    left_rows,
    right_rows,
    left_ids,
    right_ids,
    row_start,
    col_start,
    pair_target,
    hidden_bias,
    w_middle,
    w_final,
):
    panel_rows = left_rows.shape[0]
    hidden_width = left_rows.shape[1]
    pre_hidden = (
        left_rows.astype(jnp.float32)[:, None, :]
        + right_rows.astype(jnp.float32)[None, :, :]
        + hidden_bias
    )
    hidden = (
        jax.nn.silu(pre_hidden).astype(jnp.bfloat16).reshape(panel_rows * panel_rows, hidden_width)
    )
    pre_upper = jnp.dot(hidden, w_middle, preferred_element_type=jnp.float32)
    upper_act = jax.nn.silu(pre_upper)
    predicted = jnp.sum(upper_act * w_final, axis=1)
    left_pos = row_start + jnp.arange(panel_rows, dtype=jnp.int32)
    right_pos = col_start + jnp.arange(panel_rows, dtype=jnp.int32)
    same_cluster = (left_ids[:, None] == right_ids[None, :]) & (
        left_pos[:, None] != right_pos[None, :]
    )
    residual = jnp.where(same_cluster.reshape(-1), predicted - pair_target, 0.0)
    pair_slope = 16.0 * residual
    grad_final = jnp.sum(upper_act * pair_slope[:, None], axis=0)
    grad_second = (pair_slope[:, None] * w_final[None, :] * silu_slope(pre_upper)).astype(
        jnp.bfloat16
    )
    grad_middle = lax.dot_general(
        hidden, grad_second, (((0,), (0,)), ((), ())), preferred_element_type=jnp.float32
    )
    grad_hidden = lax.dot_general(
        grad_second, w_middle, (((1,), (1,)), ((), ())), preferred_element_type=jnp.float32
    )
    grad_first = grad_hidden.reshape(panel_rows, panel_rows, hidden_width) * silu_slope(pre_hidden)
    return (
        jnp.sum(grad_first, axis=1),
        jnp.sum(grad_first, axis=0),
        jnp.sum(grad_first, axis=(0, 1)),
        grad_middle,
        grad_final,
    )


def local(
    embeddings,
    cluster_ids,
    block_list,
    block_counts,
    pair_targets,
    w_left,
    w_right,
    hidden_bias,
    w_middle,
    w_final,
):
    local_emb = embeddings[0]
    whole_emb, group_ids = (
        lax.all_gather(embeddings, "blk", axis=1, tiled=True),
        lax.all_gather(cluster_ids, "blk", axis=1, tiled=True),
    )
    whole_emb = whole_emb[0]

    def fetch_panels(row_start, col_start):
        row_emb = lax.dynamic_slice_in_dim(whole_emb, row_start, PANEL, 0)
        col_emb = lax.dynamic_slice_in_dim(whole_emb, col_start, PANEL, 0)
        return (
            jnp.dot(row_emb, w_left, preferred_element_type=jnp.float32).astype(jnp.bfloat16),
            jnp.dot(col_emb, w_right, preferred_element_type=jnp.float32).astype(jnp.bfloat16),
        )

    group_ids = group_ids[0]
    local_blocks = block_list[0]
    local_targets = pair_targets[0]
    molecules = group_ids.shape[0]
    hidden_width = w_left.shape[1]

    def slot_step(slot, carry):
        part_left, part_right, sum_bias, sum_middle, sum_final = carry
        entry = lax.dynamic_index_in_dim(local_blocks, slot, 0, keepdims=False)
        row_start = entry[0] * PANEL
        col_start = entry[1] * PANEL
        pair_target = lax.dynamic_index_in_dim(local_targets, slot, 0, keepdims=False)
        left_rows, right_rows = fetch_panels(row_start, col_start)
        grad_rows, grad_cols, grad_bias, grad_middle, grad_final = pair_block(
            left_rows,
            right_rows,
            lax.dynamic_slice_in_dim(group_ids, row_start, PANEL, 0),
            lax.dynamic_slice_in_dim(group_ids, col_start, PANEL, 0),
            row_start,
            col_start,
            pair_target,
            hidden_bias,
            w_middle,
            w_final,
        )
        current = lax.dynamic_slice_in_dim(part_left, row_start, PANEL, 0)
        part_left = lax.dynamic_update_slice_in_dim(part_left, current + grad_rows, row_start, 0)
        current = lax.dynamic_slice_in_dim(part_right, col_start, PANEL, 0)
        part_right = lax.dynamic_update_slice_in_dim(part_right, current + grad_cols, col_start, 0)
        return (
            part_left,
            part_right,
            sum_bias + grad_bias,
            sum_middle + grad_middle,
            sum_final + grad_final,
        )

    empty = jnp.zeros((molecules, hidden_width), jnp.float32)
    start_state = (
        empty,
        empty,
        jnp.zeros((hidden_width,), jnp.float32),
        jnp.zeros(w_middle.shape, jnp.float32),
        jnp.zeros(w_final.shape, jnp.float32),
    )
    part_left, part_right, sum_bias, sum_middle, sum_final = lax.fori_loop(
        0, block_counts[0, 0], slot_step, start_state
    )
    rounded_left = part_left.astype(jnp.bfloat16)
    rounded_right = part_right.astype(jnp.bfloat16)
    own_left, own_right = (
        lax.psum_scatter(
            rounded_left.astype(jnp.float32).astype(jnp.bfloat16),
            "blk",
            scatter_dimension=0,
            tiled=True,
        ).astype(jnp.float32),
        lax.psum_scatter(
            rounded_right.astype(jnp.float32).astype(jnp.bfloat16),
            "blk",
            scatter_dimension=0,
            tiled=True,
        ).astype(jnp.float32),
    )
    left_grad = own_left.astype(jnp.bfloat16)
    right_grad = own_right.astype(jnp.bfloat16)
    grad_local = jnp.dot(left_grad, w_left.T, preferred_element_type=jnp.float32) + jnp.dot(
        right_grad, w_right.T, preferred_element_type=jnp.float32
    )
    weight_left = lax.dot_general(
        local_emb, left_grad, (((0,), (0,)), ((), ())), preferred_element_type=jnp.float32
    )
    weight_right = lax.dot_general(
        local_emb, right_grad, (((0,), (0,)), ((), ())), preferred_element_type=jnp.float32
    )
    summed = lax.psum((weight_left, weight_right, sum_bias, sum_middle, sum_final), ("grp", "blk"))
    devices = lax.axis_size("grp") * lax.axis_size("blk")
    scale = 1.0 / math.sqrt(devices * B_DEV * PANEL)
    return (
        grad_local[None],
        summed[0] * scale,
        summed[1] * scale,
        summed[2] * scale,
        summed[3] * scale,
        summed[4] * scale,
    )


def solution(mesh):
    return jax.shard_map(
        local,
        mesh=mesh,
        in_specs=(
            P("grp", "blk", None),
            P("grp", "blk"),
            P("grp", "blk", None),
            P("grp", "blk"),
            P("grp", "blk", None),
            P(),
            P(),
            P(),
            P(),
            P(),
        ),
        out_specs=(P("grp", "blk", None), P(), P(), P(), P(), P()),
        check_vma=False,
    )
```

profile of v0, /device:TPU:2, one launch (start us, length us, event | category | flops | bytes accessed | tf_op | source)
XLA Modules:
  0.0 784.3 jit_solution(16809696372307641489)
XLA Ops:
  7.2 0.7 all-gather.2.cloned.1.call-update
  7.9 1.3 dynamic-slice
  9.9 0.8 bitcast_dynamic-update-slice_fusion
  10.7 15.9 %all-reduce = s32[2048]{0:T(1024)S(1)} all-reduce(s32[2048]{0:T(1024)S(1)} %bitcast_dynamic-update-slice_fusion), channel_id=1, replica_groups=mesh['grp'=8,'blk'=32] {'blk'}, use_global_device_ids=true, to_apply=%add | all-reduce | flops 2048 | bytes 16384 | tf_op jit(solution)/shard_map/squeeze | solution.py:95
  26.5 37.7 %all-gather.2.cloned.1.call-done = bf16[1,2048,1024]{2,1,0:T(8,128)(2,1)} async-done(((bf16[1,64,1024]{2,1,0:T(8,128)(2,1)}), bf16[1,2048,1024]{2,1,0:T(8,128)(2,1)}) %all-gather.2.cloned.1.call-update) | async-done | bytes 4194320 | tf_op jit(solution)/shard_map/all_gather | solution.py:82
  64.3 2.5 broadcast_in_dim.14
  66.7 2.5 broadcast_in_dim.14.clone
  69.2 0.7 broadcast_in_dim.16
  70.0 60.5 %while.18 = (s32[]{:T(128)}, f32[2048,512]{1,0:T(8,128)}, f32[2048,512]{1,0:T(8,128)}, f32[512]{0:T(512)S(1)}, f32[512,128]{1,0:T(8,128)}, /*index=5*/f32[128]{0...) while((s32[]{:T(128)}, f32[2048,512]{1,0:T(8,128)}, ...), condition=%wide.region_6.7_spmd, body=%wide.region_0.6_spmd.sunk | while | flops 1822642304 | bytes 153014800 | solution.py:140
  71.9 1.2 fusion.50
  73.7 1.6 fusion.49
  75.3 1.1 broadcast_add_fusion.2
  76.5 3.4 multiply_convert_fusion.7
  79.9 1.3 multiply_reduce_fusion.6
  81.2 0.6 copy-done.2
  82.1 0.9 constant_dynamic-slice_fusion.5
  83.1 5.0 convolution_add_fusion.3
  88.1 5.3 multiply_reduce_fusion.7
  93.4 3.9 fusion.52
  97.3 1.7 add_dynamic-update-slice_fusion.3
  99.1 0.7 multiply_reduce_fusion.8
  100.5 0.5 fusion.48
  101.7 1.2 fusion.50
  103.6 1.6 fusion.49
  105.2 1.1 broadcast_add_fusion.2
  106.3 3.4 multiply_convert_fusion.7
  109.7 1.3 multiply_reduce_fusion.6
  111.1 0.6 copy-done.2
  112.0 0.9 constant_dynamic-slice_fusion.5
  112.9 5.0 convolution_add_fusion.3
  118.0 5.3 multiply_reduce_fusion.7
  123.2 3.9 fusion.52
  127.2 1.7 add_dynamic-update-slice_fusion.3
  128.9 0.7 multiply_reduce_fusion.8
  130.5 3.8 convert_element_type.34
  134.3 3.8 convert_element_type.33
  138.2 261.0 %reduce-scatter.5.cloned.1.call-done = bf16[64,512]{1,0:T(8,128)(2,1)} async-done(((bf16[2048,512]{1,0:T(8,128)(2,1)}), bf16[64,512]{1,0:T(8,128)(2,1)}) %reduce-scatter.5.cloned.1.call-update) | async-done | bytes 65552 | tf_op jit(solution)/shard_map/reduce_scatter | solution.py:152
  399.2 2.6 convolution_bitcast_fusion
  401.8 87.8 %reduce-scatter.3.cloned.1.call-done = bf16[64,512]{1,0:T(8,128)(2,1)} async-done(((bf16[2048,512]{1,0:T(8,128)(2,1)}), bf16[64,512]{1,0:T(8,128)(2,1)}) %reduce-scatter.3.cloned.1.call-update) | async-done | bytes 65552 | tf_op jit(solution)/shard_map/reduce_scatter | solution.py:146
  489.6 2.7 convolution_bitcast_fusion.1
  492.3 73.9 %all-reduce.1 = (f32[512]{0:T(512)S(1)}, f32[128]{0:T(128)S(1)}) all-reduce(f32[512]{0:T(512)S(1)} %get-tuple-element.95, f32[128]{0:T(128)S(1)} %get-tuple-element.97), channel_id=1, replica_groups=mesh['grp'=8,'blk'=32] {'grp','blk'}, use_global_device_ids=true, to_apply=%region_11.12 | all-reduce | flops 640 | bytes 5120 | tf_op jit(solution)/shard_map/psum | solution.py:170
  566.7 0.6 broadcast_multiply_fusion.3
  567.7 2.4 fusion.8
  570.1 198.0 %all-reduce.5.cloned.1.call-done = (f32[1024,512]{0,1:T(8,128)}, f32[1024,512]{0,1:T(8,128)}, f32[512,128]{1,0:T(8,128)}) async-done(((f32[1024,512]{0,1:T(8,128)}, f32[1024,512]{0,1:T(8,128)}, f32[512,128]{1,0:T(8,128)}), (f32[1024,512]{0,1:T(8,128)}, f32[1024,512]{0,1:T(8,128)}, f32[512,128]{1,0:T(8,128)})) %all-reduce.5.cloned.1.call-update) | async-done | bytes 4456464 | tf_op jit(solution)/shard_map/psum | solution.py:170
  768.1 4.2 broadcast_multiply_fusion
  772.3 2.9 copy.16
  775.2 1.8 copy.17
  777.0 0.7 broadcast_multiply_fusion.2
  (65 shorter events, 2.5 us)
Async XLA Ops:
  7.2 57.1 %all-gather.2.cloned.1.call-start = ((), (), s32[]{:S(2)}) async-start(), calls=%async_computation.2 | async-start | bytes 4325376 | tf_op jit(solution)/shard_map/all_gather | solution.py:82
  7.9 391.3 %reduce-scatter.5.cloned.1.call-start = ((), (), s32[]{:S(2)}) async-start(), calls=%async_computation.4 | async-start | bytes 2162688 | tf_op jit(solution)/shard_map/reduce_scatter | solution.py:152
  64.2 5.7 copy-start.3
  64.3 5.7 copy-start.8
  64.3 5.7 copy-start.9
  64.3 5.7 copy-start.12
  76.5 3.4 copy-start
  76.5 3.4 copy-start.10
  79.9 2.0 copy-start.2
  83.1 5.1 copy-start.1
  83.1 5.1 copy-start.11
  106.3 3.4 copy-start
  106.3 3.4 copy-start.10
  109.7 2.0 copy-start.2
  112.9 5.1 copy-start.1
  112.9 5.1 copy-start.11
  134.3 355.3 %reduce-scatter.3.cloned.1.call-start = ((), (), s32[]{:S(2)}) async-start(), calls=%async_computation.3 | async-start | bytes 2162688 | tf_op jit(solution)/shard_map/reduce_scatter | solution.py:146
  134.3 264.9 %copy-start.4 = (bf16[1,64,1024]{2,1,0:T(8,128)(2,1)S(1)}, bf16[1,64,1024]{2,1,0:T(8,128)(2,1)}, u32[]{:S(2)}) copy-start(bf16[1,64,1024]{2,1,0:T(8,128)(2,1)} %param.12) | copy-start | bytes 393220
  138.2 629.9 %all-reduce.5.cloned.1.call-start = ((), (), s32[]{:S(2)}) async-start(), calls=%async_computation.5 | async-start | bytes 8912896 | tf_op jit(solution)/shard_map/psum | solution.py:170
  401.8 165.9 %copy-start.5 = (bf16[64,512]{1,0:T(8,128)(2,1)S(1)}, bf16[64,512]{1,0:T(8,128)(2,1)}, u32[]{:S(2)}) copy-start(bf16[64,512]{1,0:T(8,128)(2,1)} %reduce-scatter.5.cloned.1.call-done) | copy-start | bytes 196612
  489.6 77.7 %copy-start.7 = (bf16[64,512]{1,0:T(8,128)(2,1)S(1)}, bf16[64,512]{1,0:T(8,128)(2,1)}, u32[]{:S(2)}) copy-start(bf16[64,512]{1,0:T(8,128)(2,1)} %reduce-scatter.3.cloned.1.call-done) | copy-start | bytes 196612
  772.3 4.7 copy-start.6
Sparse Core Ops, SparseCore 0:
  10.5 53.6 all-gather.1
  134.4 264.7 reduce-scatter.4
  403.6 85.9 reduce-scatter.2
  495.8 272.2 all-reduce.4
where the time goes:
time: 786 us; the launch traced here: 784 us
  waiting for transfers between devices  585 us (74%)
  blocking collectives  89.8 us (11%)
  matrix products  37 us (5%)
  other arithmetic  35.6 us (5%)
  local copies, waits for them, and re-layouts  17.1 us (2%)
  between operations  14.5 us (2%)
    reduce_scatter x1, waiting for transfers between devices, local(): lax.psum_scatter(rounded_right.astype(jnp.float32).astype(jnp.bfloat16),...  261 us
    psum x1, waiting for transfers between devices, local(): lax.psum((weight_left, weight_right, sum_bias, sum_middle, sum_final), ('...  198 us
    reduce_scatter x1, waiting for transfers between devices, local(): lax.psum_scatter(rounded_left.astype(jnp.float32).astype(jnp.bfloat16), '...  87.8 us
    psum x1, blocking collectives, local(): lax.psum((weight_left, weight_right, sum_bias, sum_middle, sum_final), ('...  73.9 us
    all_gather x1, waiting for transfers between devices, local(): lax.all_gather(embeddings, 'blk', axis=1, tiled=True)  37.7 us
    squeeze x1, blocking collectives, local(): group_ids = group_ids[0]  15.9 us
  transfers between devices with their start and end apart: 4, of which 4 were waited for; matrix products, arithmetic and copies ran while one was open for 2% of the time, Pallas kernels for 0%

commit v1 on v0

--- a/solution.py
+++ b/solution.py
@@ -167,7 +167,9 @@
     weight_right = lax.dot_general(
         local_emb, right_grad, (((0,), (0,)), ((), ())), preferred_element_type=jnp.float32
     )
-    summed = lax.psum((weight_left, weight_right, sum_bias, sum_middle, sum_final), ("grp", "blk"))
+    summed = lax.psum(
+        lax.psum((weight_left, weight_right, sum_bias, sum_middle, sum_final), "grp"), "blk"
+    )
     devices = lax.axis_size("grp") * lax.axis_size("blk")
     scale = 1.0 / math.sqrt(devices * B_DEV * PANEL)
     return (

time: 786 us -> 749 us (0.953)
  waiting for transfers between devices: 585 us -> 548 us
    psum x1 -> x2, waiting for transfers between devices: 198 us -> 160 us  [the longest x1 114 us: local(): lax.psum((weight_left, weight_right, sum_bias, sum_middle, sum_final), 'g...]
    psum x1 -> x2, blocking collectives: 73.9 us -> 73.9 us  [the longest x1 58.4 us: local(): lax.psum(lax.psum((weight_left, weight_right, sum_bias, sum_middle, sum_f...]
  transfers between devices with their start and end apart: 4 -> 5, of which waited for: 4 -> 5; matrix products, arithmetic and copies ran while one was open for 2% -> 2% of each run, Pallas kernels for 0% -> 0%
where the time goes in v1:
time: 749 us; the launch traced here: 747 us
  waiting for transfers between devices  548 us (73%)
  blocking collectives  89.8 us (12%)
  matrix products  36.9 us (5%)
  other arithmetic  35.6 us (5%)
  local copies, waits for them, and re-layouts  17.1 us (2%)
  between operations  14.5 us (2%)
    reduce_scatter x1, waiting for transfers between devices, local(): lax.psum_scatter(rounded_right.astype(jnp.float32).astype(jnp.bfloat16),...  261 us
    psum x1, waiting for transfers between devices, local(): lax.psum((weight_left, weight_right, sum_bias, sum_middle, sum_final), 'g...  114 us
    reduce_scatter x1, waiting for transfers between devices, local(): lax.psum_scatter(rounded_left.astype(jnp.float32).astype(jnp.bfloat16), '...  87.8 us
    psum x1, blocking collectives, local(): lax.psum(lax.psum((weight_left, weight_right, sum_bias, sum_middle, sum_f...  58.4 us
    psum x1, waiting for transfers between devices, local(): lax.psum(lax.psum((weight_left, weight_right, sum_bias, sum_middle, sum_f...  46.4 us
    all_gather x1, waiting for transfers between devices, local(): lax.all_gather(embeddings, 'blk', axis=1, tiled=True)  37.7 us
    squeeze x1, blocking collectives, local(): group_ids = group_ids[0]  15.9 us
    psum x1, blocking collectives, local(): lax.psum((weight_left, weight_right, sum_bias, sum_middle, sum_final), 'g...  15.5 us
  transfers between devices with their start and end apart: 5, of which 5 were waited for; matrix products, arithmetic and copies ran while one was open for 2% of the time, Pallas kernels for 0%

profile of v1, /device:TPU:2, one launch (start us, length us, event | category | flops | bytes accessed | tf_op | source)
XLA Modules:
  0.0 746.8 jit_solution(6427941696506572078)
XLA Ops:
  7.2 0.7 all-gather.2.cloned.1.call-update
  7.9 1.3 dynamic-slice
  9.9 0.8 bitcast_dynamic-update-slice_fusion
  10.7 15.9 %all-reduce = s32[2048]{0:T(1024)S(1)} all-reduce(s32[2048]{0:T(1024)S(1)} %bitcast_dynamic-update-slice_fusion), channel_id=1, replica_groups=mesh['grp'=8,'blk'=32] {'blk'}, use_global_device_ids=true, to_apply=%add | all-reduce | flops 2048 | bytes 16384 | tf_op jit(solution)/shard_map/squeeze | solution.py:95
  26.5 37.7 %all-gather.2.cloned.1.call-done = bf16[1,2048,1024]{2,1,0:T(8,128)(2,1)} async-done(((bf16[1,64,1024]{2,1,0:T(8,128)(2,1)}), bf16[1,2048,1024]{2,1,0:T(8,128)(2,1)}) %all-gather.2.cloned.1.call-update) | async-done | bytes 4194320 | tf_op jit(solution)/shard_map/all_gather | solution.py:82
  64.3 2.5 broadcast_in_dim.14
  66.7 2.5 broadcast_in_dim.14.clone
  69.2 0.7 broadcast_in_dim.16
  70.0 60.5 %while.18 = (s32[]{:T(128)}, f32[2048,512]{1,0:T(8,128)}, f32[2048,512]{1,0:T(8,128)}, f32[512]{0:T(512)S(1)}, f32[512,128]{1,0:T(8,128)}, /*index=5*/f32[128]{0...) while((s32[]{:T(128)}, f32[2048,512]{1,0:T(8,128)}, ...), condition=%wide.region_6.7_spmd, body=%wide.region_0.6_spmd.sunk | while | flops 1822642304 | bytes 153014800 | solution.py:140
  71.9 1.2 fusion.50
  73.7 1.6 fusion.49
  75.3 1.1 broadcast_add_fusion.2
  76.5 3.4 multiply_convert_fusion.7
  79.9 1.3 multiply_reduce_fusion.6
  81.2 0.6 copy-done.2
  82.1 0.9 constant_dynamic-slice_fusion.5
  83.1 5.0 convolution_add_fusion.3
  88.1 5.3 multiply_reduce_fusion.7
  93.4 3.9 fusion.52
  97.3 1.7 add_dynamic-update-slice_fusion.3
  99.1 0.7 multiply_reduce_fusion.8
  101.7 1.2 fusion.50
  103.6 1.6 fusion.49
  105.2 1.1 broadcast_add_fusion.2
  106.3 3.4 multiply_convert_fusion.7
  109.7 1.3 multiply_reduce_fusion.6
  111.1 0.6 copy-done.2
  112.0 0.9 constant_dynamic-slice_fusion.5
  112.9 5.0 convolution_add_fusion.3
  118.0 5.3 multiply_reduce_fusion.7
  123.2 3.9 fusion.52
  127.2 1.7 add_dynamic-update-slice_fusion.3
  128.9 0.7 multiply_reduce_fusion.8
  130.5 3.8 convert_element_type.34
  134.3 3.8 convert_element_type.33
  138.2 261.0 %reduce-scatter.5.cloned.1.call-done = bf16[64,512]{1,0:T(8,128)(2,1)} async-done(((bf16[2048,512]{1,0:T(8,128)(2,1)}), bf16[64,512]{1,0:T(8,128)(2,1)}) %reduce-scatter.5.cloned.1.call-update) | async-done | bytes 65552 | tf_op jit(solution)/shard_map/reduce_scatter | solution.py:152
  399.2 2.6 convolution_bitcast_fusion
  401.8 87.8 %reduce-scatter.3.cloned.1.call-done = bf16[64,512]{1,0:T(8,128)(2,1)} async-done(((bf16[2048,512]{1,0:T(8,128)(2,1)}), bf16[64,512]{1,0:T(8,128)(2,1)}) %reduce-scatter.3.cloned.1.call-update) | async-done | bytes 65552 | tf_op jit(solution)/shard_map/reduce_scatter | solution.py:146
  489.6 2.6 convolution_bitcast_fusion.1
  492.3 114.0 %all-reduce.10.cloned.1.call-done = (f32[1024,512]{0,1:T(8,128)}, f32[1024,512]{0,1:T(8,128)}, f32[512,128]{1,0:T(8,128)}) async-done(((f32[1024,512]{0,1:T(8,128)}, f32[1024,512]{0,1:T(8,128)}, f32[512,128]{1,0:T(8,128)}), (f32[1024,512]{0,1:T(8,128)}, f32[1024,512]{0,1:T(8,128)}, f32[512,128]{1,0:T(8,128)})) %all-reduce.10.cloned.1.call-update) | async-done | bytes 4456464 | tf_op jit(solution)/shard_map/psum | solution.py:171
  606.3 15.5 %all-reduce.3 = (f32[512]{0:T(512)S(1)}, f32[128]{0:T(128)S(1)}) all-reduce(f32[512]{0:T(512)S(1)} %get-tuple-element.95, f32[128]{0:T(128)S(1)} %get-tuple-element.97), channel_id=1, replica_groups=mesh['grp'=8,'blk'=32] {'grp'}, use_global_device_ids=true, to_apply=%region_13.14 | all-reduce | flops 640 | bytes 5120 | tf_op jit(solution)/shard_map/psum | solution.py:171
  621.9 58.4 %all-reduce.1 = (f32[512]{0:T(512)S(1)}, f32[128]{0:T(128)S(1)}) all-reduce(f32[512]{0:T(512)S(1)} %get-tuple-element.143, f32[128]{0:T(128)S(1)} %get-tuple-element.144), channel_id=1, replica_groups=mesh['grp'=8,'blk'=32] {'blk'}, use_global_device_ids=true, to_apply=%region_14.15 | all-reduce | flops 640 | bytes 5120 | tf_op jit(solution)/shard_map/psum | solution.py:170
  681.8 2.4 fusion.8
  684.2 46.4 %all-reduce.8.cloned.1.call-done = (f32[1024,512]{0,1:T(8,128)}, f32[1024,512]{0,1:T(8,128)}, f32[512,128]{1,0:T(8,128)}) async-done(((f32[1024,512]{0,1:T(8,128)}, f32[1024,512]{0,1:T(8,128)}, f32[512,128]{1,0:T(8,128)}), (f32[1024,512]{0,1:T(8,128)}, f32[1024,512]{0,1:T(8,128)}, f32[512,128]{1,0:T(8,128)})) %all-reduce.8.cloned.1.call-update) | async-done | bytes 4456464 | tf_op jit(solution)/shard_map/psum | solution.py:170
  730.6 4.2 broadcast_multiply_fusion
  734.8 2.9 copy.16
  737.8 1.8 copy.17
  739.6 0.7 broadcast_multiply_fusion.2
  (69 shorter events, 3.6 us)
Async XLA Ops:
  7.2 57.1 %all-gather.2.cloned.1.call-start = ((), (), s32[]{:S(2)}) async-start(), calls=%async_computation.2 | async-start | bytes 4325376 | tf_op jit(solution)/shard_map/all_gather | solution.py:82
  7.9 391.3 %reduce-scatter.5.cloned.1.call-start = ((), (), s32[]{:S(2)}) async-start(), calls=%async_computation.4 | async-start | bytes 2162688 | tf_op jit(solution)/shard_map/reduce_scatter | solution.py:152
  64.2 5.7 copy-start.3
  64.3 5.7 copy-start.8
  64.3 5.7 copy-start.9
  64.3 5.7 copy-start.12
  76.5 3.4 copy-start
  76.5 3.4 copy-start.10
  79.9 2.0 copy-start.2
  83.1 5.1 copy-start.1
  83.1 5.1 copy-start.11
  106.3 3.4 copy-start
  106.3 3.4 copy-start.10
  109.7 2.0 copy-start.2
  112.9 5.1 copy-start.1
  112.9 5.1 copy-start.11
  134.3 355.3 %reduce-scatter.3.cloned.1.call-start = ((), (), s32[]{:S(2)}) async-start(), calls=%async_computation.3 | async-start | bytes 2162688 | tf_op jit(solution)/shard_map/reduce_scatter | solution.py:146
  134.3 264.9 %copy-start.4 = (bf16[1,64,1024]{2,1,0:T(8,128)(2,1)S(1)}, bf16[1,64,1024]{2,1,0:T(8,128)(2,1)}, u32[]{:S(2)}) copy-start(bf16[1,64,1024]{2,1,0:T(8,128)(2,1)} %param.12) | copy-start | bytes 393220
  138.2 468.2 %all-reduce.10.cloned.1.call-start = ((), (), s32[]{:S(2)}) async-start(), calls=%async_computation.6 | async-start | bytes 8912896 | tf_op jit(solution)/shard_map/psum | solution.py:171
  492.2 189.1 %copy-start.7 = (bf16[64,512]{1,0:T(8,128)(2,1)S(1)}, bf16[64,512]{1,0:T(8,128)(2,1)}, u32[]{:S(2)}) copy-start(bf16[64,512]{1,0:T(8,128)(2,1)} %reduce-scatter.3.cloned.1.call-done) | copy-start | bytes 196612
  492.2 189.6 %copy-start.5 = (bf16[64,512]{1,0:T(8,128)(2,1)S(1)}, bf16[64,512]{1,0:T(8,128)(2,1)}, u32[]{:S(2)}) copy-start(bf16[64,512]{1,0:T(8,128)(2,1)} %reduce-scatter.5.cloned.1.call-done) | copy-start | bytes 196612
  492.2 238.4 %all-reduce.8.cloned.1.call-start = ((), (), s32[]{:S(2)}) async-start(), calls=%async_computation.5 | async-start | bytes 8912896 | tf_op jit(solution)/shard_map/psum | solution.py:170
  734.8 4.7 copy-start.6
Sparse Core Ops, SparseCore 0:
  10.5 53.6 all-gather.1
  134.4 264.7 reduce-scatter.4
  403.6 85.9 reduce-scatter.2
  492.6 113.6 all-reduce.9
  609.9 120.6 all-reduce.7
